TPU v7x, 32 devices: a whole 2x2x4 slice. The times are simulated.
32 devices in a mesh: seq: 16 (over z, x, core), ch: 2 (over y).
Axes of the slice: x: 2, y: 2, z: 4, core: 2. Of those that a mesh axis runs over, the one named last changes fastest.
Arguments:
- query_feat: bfloat16 [4096, 4096], P('seq', 'ch'), may hold values from -6 to 6
- key_feat: bfloat16 [4096, 4096], P('seq', 'ch'), may hold values from -6 to 6
- value_feat: bfloat16 [4096, 4096], P('seq', 'ch'), may hold values from -6 to 6
- short_filter: float32 [3, 3, 4096], P(None, None, 'ch'), may hold values from -3.5 to 3.5
- long_filter: float32 [2048, 4096], P('ch', 'seq'), may hold values from -0.09375 to 0.09375
- direct_gain: float32 [4096], P('ch'), may hold values from 0.25 to 1.5
- out_weight: bfloat16 [4096, 4096], P('seq', 'ch'), may hold values from -0.09375 to 0.09375
Outputs:
- layer_out: bfloat16 [4096, 4096], P('seq', 'ch')
All inputs are finite; a program needn't handle non-finite values.
Results may differ from a plain program's by a relative error of at most 0.0049.
Values may be sent and summed in bfloat16 or wider, within the bound.
No kernel may reach another device: no remote copies, remote signals or barrier semaphores. Data moves between devices by JAX's collectives and lax.ppermute only.
A program may use at most 64 MiB of HBM per device.

v0:
```python
import math

import jax
import jax.numpy as jnp
from jax import lax
from jax.sharding import PartitionSpec as P

TAPS = 3


highest = lax.Precision.HIGHEST


def shifted(block, axis, distance):
    devices = range(lax.axis_size(axis))
    route = [(i - distance, i) for i in devices if i - distance in devices]
    return lax.ppermute(block, axis, route)


def angles(row_index, col_index, period, direction):
    product = row_index[:, None] * col_index[None, :] % period
    phase_angle = direction * 2.0 * math.pi / period * product.astype(jnp.float32)
    return (jnp.cos(phase_angle), jnp.sin(phase_angle))


def complex_apply(real_part, imag_part, table_real, table_imag, formula):

    def contract(operand_one, operand_two):
        return jnp.einsum(formula, operand_one, operand_two, precision=highest)

    out_real = contract(real_part, table_real) - contract(imag_part, table_imag)
    out_imag = contract(real_part, table_imag) + contract(imag_part, table_real)
    return (out_real, out_imag)


def multiply(operand_one, operand_two):
    return jnp.stack(
        [
            operand_one[0] * operand_two[0] - operand_one[1] * operand_two[1],
            operand_one[0] * operand_two[1] + operand_one[1] * operand_two[0],
        ]
    )


def local(query_feat, key_feat, value_feat, short_filter, long_filter, direct_gain, out_weight):
    tokens, channels = query_feat.shape
    devices = lax.axis_size("seq")
    total_len = 2 * devices * tokens
    tok_index = jnp.arange(tokens, dtype=jnp.int32)
    pos_index = jnp.arange(devices, dtype=jnp.int32)
    conv_edge = jnp.stack(
        [
            query_feat[tokens - (TAPS - 1) :],
            key_feat[tokens - (TAPS - 1) :],
            value_feat[tokens - (TAPS - 1) :],
        ]
    )
    before = shifted(conv_edge, "seq", 1)

    def featurize(index, inputs):
        rows = jnp.concatenate([before[index], inputs], axis=0).astype(jnp.float32)
        total = jnp.zeros((tokens, channels), jnp.float32)
        for tap in range(TAPS):
            total = (
                total + short_filter[index, tap] * rows[TAPS - 1 - tap : TAPS - 1 - tap + tokens]
            )
        return total

    query_short = featurize(0, query_feat)
    mixed = featurize(1, key_feat) * featurize(2, value_feat)
    spread_data = lax.all_to_all(mixed, "seq", split_axis=1, concat_axis=0, tiled=True)
    spread_filter = lax.all_to_all(long_filter, "seq", split_axis=0, concat_axis=1, tiled=True)
    local_pairs = spread_filter.shape[0]
    grid = spread_data.reshape(devices, tokens, local_pairs, 2).transpose(3, 2, 0, 1)
    filter_grid = spread_filter.reshape(local_pairs, devices, tokens)
    in_real = jnp.concatenate([grid[0], filter_grid], axis=0)
    in_imag = jnp.concatenate([grid[1], jnp.zeros_like(filter_grid)], axis=0)
    wide = 2 * devices
    wide_index = jnp.arange(wide, dtype=jnp.int32)
    step_real, step_imag = angles(pos_index, wide_index, wide, -1.0)
    part_real, part_imag = complex_apply(in_real, in_imag, step_real, step_imag, "spn,pk->skn")
    twiddle_real, twiddle_imag = angles(wide_index, tok_index, total_len, -1.0)
    turned_real = part_real * twiddle_real - part_imag * twiddle_imag
    turned_imag = part_real * twiddle_imag + part_imag * twiddle_real
    fine_real, fine_imag = angles(tok_index, tok_index, tokens, -1.0)
    spec_real, spec_imag = complex_apply(
        turned_real, turned_imag, fine_real, fine_imag, "skn,nm->skm"
    )
    filtered = multiply(
        (spec_real[:local_pairs], spec_imag[:local_pairs]),
        (spec_real[local_pairs:], spec_imag[local_pairs:]),
    )
    back_real, back_imag = angles(tok_index, tok_index, tokens, 1.0)
    inv_real, inv_imag = complex_apply(
        filtered[0], filtered[1], back_real, back_imag, "skm,mn->skn"
    )
    untwist_real, untwist_imag = angles(wide_index, tok_index, total_len, 1.0)
    again_real = inv_real * untwist_real - inv_imag * untwist_imag
    again_imag = inv_real * untwist_imag + inv_imag * untwist_real
    last_real, last_imag = angles(wide_index, pos_index, wide, 1.0)
    out_real, out_imag = complex_apply(again_real, again_imag, last_real, last_imag, "skn,kp->spn")
    inverse_scale = 1.0 / total_len
    conv_rows = (jnp.stack([out_real, out_imag], axis=-1) * inverse_scale).transpose(1, 2, 0, 3)
    conv_rows = conv_rows.reshape(devices * tokens, 2 * local_pairs)
    long_out = lax.all_to_all(conv_rows, "seq", split_axis=0, concat_axis=1, tiled=True)
    summed = long_out + direct_gain * mixed
    gated_out = (query_short * summed).astype(jnp.bfloat16)
    features = lax.all_gather(gated_out, "ch", axis=1, tiled=True)
    result = jnp.dot(
        features,
        lax.all_gather(out_weight, "seq", axis=0, tiled=True),
        preferred_element_type=jnp.float32,
    )
    return result.astype(jnp.bfloat16)


def solution(mesh):
    in_specs = (
        P("seq", "ch"),
        P("seq", "ch"),
        P("seq", "ch"),
        P(None, None, "ch"),
        P("ch", "seq"),
        P("ch"),
        P("seq", "ch"),
    )
    out_specs = P("seq", "ch")
    return jax.shard_map(local, mesh=mesh, in_specs=in_specs, out_specs=out_specs, check_vma=False)
```

profile of v0, /device:TPU:0, one launch (start us, length us, event | category | flops | bytes accessed | tf_op | source)
XLA Modules:
  0.0 401.7 jit_solution(17259873385032809521)
XLA Ops:
  10.7 7.2 %all-to-all-start.1 = ((f32[16,64,256]{2,1,0:T(8,128)}), f32[16,64,256]{2,1,0:T(8,128)S(1)}, u32[]{:S(2)}, u32[]{:S(2)}) async-start(f32[16,64,256]{2,1,0:T(8,128)} %bitcast.106), calls=%async_computation.1 | async-start | bytes 2097152 | tf_op jit(solution)/shard_map/all_to_all | solution.py:72
  24.6 5.1 %fusion.25 = f32[256,2048]{0,1:T(8,128)} fusion(f32[258,2048]{0,1:T(8,128)S(1)} %maximum_convert_fusion.2, f32[258,2048]{0,1:T(8,128)S(1)} %maximum_convert_fusion.1, f32[2048]{0:T(1024)S(1)} %bitcast.111, f32[2048]{0:T(1024)S(1)} %bitcast.112, f32[2048]{0:T(1024)S(1)} %bitcast.107, f32[2048]{0:T(1024)S(1)} %bitcast.108, f32[2048]{0:T(1024)S(1)} %bitcast.109, ...), kind=kLoop, calls=%fused_computation.21 | loop fusion | flops 5767168 | bytes 14729216 | tf_op jit(solution)/shard_map/mul | solution.py:70
  29.7 11.1 %all-to-all-done.1 = f32[16,64,256]{2,1,0:T(8,128)S(1)} async-done(((f32[16,64,256]{2,1,0:T(8,128)}), f32[16,64,256]{2,1,0:T(8,128)S(1)}, u32[]{:S(2)}, u32[]{:S(2)}) %all-to-all-start.1) | async-done | bytes 1048608 | tf_op jit(solution)/shard_map/all_to_all | solution.py:72
  41.7 7.3 %all-to-all-start = ((f32[256,16,128]{0,2,1:T(8,128)}), f32[256,16,128]{0,2,1:T(8,128)S(1)}, u32[]{:S(2)}, u32[]{:S(2)}) async-start(f32[256,16,128]{0,2,1:T(8,128)} %bitcast.17), calls=%async_computation | async-start | bytes 4194304 | tf_op jit(solution)/shard_map/all_to_all | solution.py:71
  51.2 38.3 %all-to-all-done = f32[256,16,128]{0,2,1:T(8,128)S(1)} async-done(((f32[256,16,128]{0,2,1:T(8,128)}), f32[256,16,128]{0,2,1:T(8,128)S(1)}, u32[]{:S(2)}, u32[]{:S(2)}) %all-to-all-start) | async-done | bytes 2097184 | tf_op jit(solution)/shard_map/all_to_all | solution.py:71
  91.1 3.5 fusion.43
  94.6 3.5 fusion.42
  98.2 3.0 fusion.12
  101.1 3.6 subtract_bitcast_fusion
  104.7 6.5 %fusion.2 = f32[128,32,256]{2,0,1:T(8,128)S(1)} fusion(f32[128,32,256]{2,1,0:T(8,128)S(1)} %get-tuple-element.6), kind=kOutput, calls=%fused_computation.4 | convolution fusion | flops 3222142976 | bytes 8388608 | tf_op jit(solution)/shard_map/skn,nm->skm/dot_general | solution.py:29
  111.2 6.7 %fusion = f32[128,32,256]{2,0,1:T(8,128)S(1)} fusion(f32[128,32,256]{2,1,0:T(8,128)S(1)} %get-tuple-element.6), kind=kOutput, calls=%fused_computation.2 | convolution fusion | flops 3222142976 | bytes 8388608 | tf_op jit(solution)/shard_map/skn,nm->skm/dot_general | solution.py:29
  117.9 6.5 %fusion.18 = f32[128,32,256]{2,0,1:T(8,128)S(1)} fusion(f32[128,32,256]{2,0,1:T(8,128)S(1)} %fusion.2, f32[128,32,256]{2,1,0:T(8,128)S(1)} %get-tuple-element.5), kind=kOutput, calls=%fused_computation.17 | convolution fusion | flops 3223191552 | bytes 12582912 | tf_op jit(solution)/shard_map/skn,nm->skm/dot_general | solution.py:29
  124.3 6.9 %fusion.21 = f32[128,32,256]{2,0,1:T(8,128)S(1)} fusion(f32[128,32,256]{2,0,1:T(8,128)S(1)} %fusion, f32[128,32,256]{2,1,0:T(8,128)S(1)} %get-tuple-element.5), kind=kOutput, calls=%fused_computation.18 | convolution fusion | flops 3223191552 | bytes 12582912 | tf_op jit(solution)/shard_map/skn,nm->skm/dot_general | solution.py:29
  132.2 3.8 fusion.36
  136.1 4.0 fusion.34
  140.1 3.9 fusion.44
  144.0 3.9 fusion.47
  154.1 2.6 copy.64
  156.7 11.4 %all-to-all-start.2 = ((f32[16,256,128]{1,2,0:T(8,128)}), f32[16,256,128]{1,2,0:T(8,128)}, u32[]{:S(2)}, u32[]{:S(2)}) async-start(f32[16,256,128]{1,2,0:T(8,128)} %copy.64), calls=%async_computation.2 | async-start | bytes 4194304 | tf_op jit(solution)/shard_map/all_to_all | solution.py:105
  172.5 36.6 %all-to-all-done.2 = f32[16,256,128]{1,2,0:T(8,128)} async-done(((f32[16,256,128]{1,2,0:T(8,128)}), f32[16,256,128]{1,2,0:T(8,128)}, u32[]{:S(2)}, u32[]{:S(2)}) %all-to-all-start.2) | async-done | bytes 2097184 | tf_op jit(solution)/shard_map/all_to_all | solution.py:105
  209.1 5.1 %fusion.31 = bf16[256,2048]{0,1:T(8,128)(2,1)} fusion(f32[258,2048]{0,1:T(8,128)S(1)} %maximum_convert_fusion, f32[16,256,128]{1,2,0:T(8,128)} %all-to-all-done.2, f32[256,2048]{0,1:T(8,128)} %fusion.25, f32[2048]{0:T(1024)S(1)} %copy-done.5, f32[2048]{0:T(1024)S(1)} %bitcast.114, f32[2048]{0:T(1024)S(1)} %bitcast.115, f32[2048]{0:T(1024)S(1)} %bitcast.113), kind=kLoop, calls=%fused_computation.33 | loop fusion | flops 4718592 | bytes 11567104 | tf_op jit(solution)/shard_map/convert_element_type | solution.py:107
  215.0 39.1 %all-gather.3.cloned.1.call-done = bf16[256,4096]{0,1:T(8,128)(2,1)} async-done(((bf16[256,2048]{0,1:T(8,128)(2,1)}), bf16[256,4096]{0,1:T(8,128)(2,1)}) %all-gather.3.cloned.1.call-update) | async-done | bytes 2097168 | tf_op jit(solution)/shard_map/all_gather | solution.py:108
  254.1 128.6 %all-gather.5.cloned.1.call-done = bf16[4096,2048]{1,0:T(8,128)(2,1)} async-done(((bf16[256,2048]{1,0:T(8,128)(2,1)}), bf16[4096,2048]{1,0:T(8,128)(2,1)}) %all-gather.5.cloned.1.call-update) | async-done | bytes 16777232 | tf_op jit(solution)/shard_map/all_gather | solution.py:111
  382.7 11.9 %convolution_convert_fusion = bf16[256,2048]{1,0:T(8,128)(2,1)} fusion(bf16[256,4096]{0,1:T(8,128)(2,1)} %all-gather.3.cloned.1.call-done, bf16[4096,2048]{1,0:T(8,128)(2,1)} %all-gather.5.cloned.1.call-done), kind=kOutput, calls=%fused_computation.10 | convolution fusion | flops 4295491584 | bytes 19922944 | tf_op jit(solution)/shard_map/dot_general | solution.py:109
  (45 shorter events, 27.8 us)
Async XLA Ops:
  6.5 11.4 %copy-start.2 = (bf16[256,2048]{1,0:T(8,128)(2,1)S(1)}, bf16[256,2048]{1,0:T(8,128)(2,1)}, u32[]{:S(2)}) copy-start(bf16[256,2048]{1,0:T(8,128)(2,1)} %param.8) | copy-start | bytes 3145732
  6.5 11.3 %copy-start.4 = (f32[3,3,2048]{2,1,0:T(4,128)S(1)}, f32[3,3,2048]{2,1,0:T(4,128)}, u32[]{:S(2)}) copy-start(f32[3,3,2048]{2,1,0:T(4,128)} %param.10) | copy-start | bytes 221188
  8.3 11.7 %collective-permute-start = (bf16[3,2,2048]{2,1,0:T(2,128)(2,1)S(1)}, bf16[3,2,2048]{2,1,0:T(2,128)(2,1)S(1)}, u32[]{:S(2)}, u32[]{:S(2)}) collective-permute-start(bf16[3,2,2048]{2,1,0:T(2,128)(2,1)S(1)} %pad_maximum_fusion.3), channel_id=1, source_target_pairs={{0,2},{2,4},{4,6},{6,8},{8,10},{10,12},{12,14},{14,16},{16,18},{18... | collective-permute-start | bytes 73736 | tf_op jit(solution)/shard_map/ppermute | solution.py:17
  10.7 30.1 %all-to-all-start.1 = ((f32[16,64,256]{2,1,0:T(8,128)}), f32[16,64,256]{2,1,0:T(8,128)S(1)}, u32[]{:S(2)}, u32[]{:S(2)}) async-start(f32[16,64,256]{2,1,0:T(8,128)} %bitcast.106), calls=%async_computation.1 | async-start | bytes 2097152 | tf_op jit(solution)/shard_map/all_to_all | solution.py:72
  22.1 1.8 copy-start.1
  40.7 1.0 copy-start
  41.7 47.8 %all-to-all-start = ((f32[256,16,128]{0,2,1:T(8,128)}), f32[256,16,128]{0,2,1:T(8,128)S(1)}, u32[]{:S(2)}, u32[]{:S(2)}) async-start(f32[256,16,128]{0,2,1:T(8,128)} %bitcast.17), calls=%async_computation | async-start | bytes 4194304 | tf_op jit(solution)/shard_map/all_to_all | solution.py:71
  156.6 11.5 %copy-start.3 = (bf16[256,2048]{1,0:T(8,128)(2,1)S(1)}, bf16[256,2048]{1,0:T(8,128)(2,1)}, u32[]{:S(2)}) copy-start(bf16[256,2048]{1,0:T(8,128)(2,1)} %param.7) | copy-start | bytes 3145732
  156.7 52.4 %all-to-all-start.2 = ((f32[16,256,128]{1,2,0:T(8,128)}), f32[16,256,128]{1,2,0:T(8,128)}, u32[]{:S(2)}, u32[]{:S(2)}) async-start(f32[16,256,128]{1,2,0:T(8,128)} %copy.64), calls=%async_computation.2 | async-start | bytes 4194304 | tf_op jit(solution)/shard_map/all_to_all | solution.py:105
  168.1 86.0 %all-gather.3.cloned.1.call-start = ((), (), s32[]{:S(2)}) async-start(), calls=%async_computation.3 | async-start | bytes 3145728 | tf_op jit(solution)/shard_map/all_gather | solution.py:108
  170.5 38.6 %copy-start.5 = (f32[2048]{0:T(1024)S(1)}, f32[2048]{0:T(1024)}, u32[]{:S(2)}) copy-start(f32[2048]{0:T(1024)} %param.12) | copy-start | bytes 24580
  214.2 168.5 %all-gather.5.cloned.1.call-start = ((), (), s32[]{:S(2)}) async-start(), calls=%async_computation.4 | async-start | bytes 17825792 | tf_op jit(solution)/shard_map/all_gather | solution.py:111
Sparse Core Ops, SparseCore 0:
  214.3 39.6 all-gather.2
  256.2 126.4 all-gather.4
where the time goes:
time: 406 us; the launch traced here: 402 us
  waiting for transfers between devices  254 us (63%)
  matrix products  73.3 us (18%)
  starting transfers between devices  28.6 us (7%)
  other arithmetic  16.2 us (4%)
  local copies, waits for them, and re-layouts  15.5 us (4%)
  between operations  14 us (3%)
    all_gather x1, waiting for transfers between devices, local(): lax.all_gather(out_weight, 'seq', axis=0, tiled=True)  129 us
    dot_general x16, matrix products, contract(): return jnp.einsum(formula, operand_one, operand_two, precision=highest)  61.4 us
    all_gather x1, waiting for transfers between devices, local(): features = lax.all_gather(gated_out, 'ch', axis=1, tiled=True)  39.1 us
    all_to_all x1, waiting for transfers between devices, local(): lax.all_to_all(mixed, 'seq', split_axis=1, concat_axis=0, tiled=True)  38.3 us
    all_to_all x1, waiting for transfers between devices, local(): lax.all_to_all(conv_rows, 'seq', split_axis=0, concat_axis=1, tiled=True)  36.6 us
    dot_general x1, matrix products, local(): jnp.dot(features, lax.all_gather(out_weight, 'seq', axis=0, tiled=True),...  11.9 us
    all_to_all x1, starting transfers between devices, local(): lax.all_to_all(conv_rows, 'seq', split_axis=0, concat_axis=1, tiled=True)  11.4 us
    all_to_all x1, waiting for transfers between devices, local(): lax.all_to_all(long_filter, 'seq', split_axis=0, concat_axis=1, tiled=True)  11.1 us
  transfers between devices with their start and end apart: 6, of which 5 were waited for; matrix products, arithmetic and copies ran while one was open for 5% of the time, Pallas kernels for 0%

commit v1 on v0

v1 whole, which is shorter than its diff:
```python
import functools

import jax
import jax.numpy as jnp
from jax import lax
from jax.experimental import pallas as pl
from jax.experimental.pallas import tpu as pltpu
from jax.sharding import PartitionSpec as P


TAPS = 3
LANES = 128
PACK = 16


def shifted(block, axis, distance):
    devices = range(lax.axis_size(axis))
    route = [(i - distance, i) for i in devices if i - distance in devices]
    return lax.ppermute(block, axis, route)


def featurized(inputs, edge, taps):
    rows = inputs.astype(jnp.float32)
    index = lax.broadcasted_iota(jnp.int32, rows.shape, 0)
    total = taps[0:1] * rows
    for tap in range(1, TAPS):
        moved = pltpu.roll(rows, tap, 0)
        for row in range(tap):
            first = TAPS - 1 - tap + row
            moved = jnp.where(index == row, edge[first : first + 1], moved)
        total = total + taps[tap : tap + 1] * moved
    return total


def mix_kernel(key_ref, value_ref, edge_ref, short_ref, mixed_ref, turned_ref):
    edge = edge_ref[...].astype(jnp.float32)
    mixed = featurized(key_ref[...], edge[1], short_ref[1]) * featurized(
        value_ref[...], edge[2], short_ref[2]
    )
    mixed_ref[...] = mixed
    turned_ref[...] = mixed.T.astype(jnp.bfloat16)


def gate_kernel(query_ref, edge_ref, short_ref, gain_ref, mixed_ref, conv_ref, gated_ref):
    edge = edge_ref[...].astype(jnp.float32)
    query_short = featurized(query_ref[...], edge[0], short_ref[0])
    summed = conv_ref[...].astype(jnp.float32).T + gain_ref[...] * mixed_ref[...]
    gated_ref[...] = (query_short * summed).astype(jnp.bfloat16)


def conv_kernel(n, tok, width, x_ref, f_ref, y_ref, xi, xs, ys):
    halves = tok // LANES
    groups = LANES // PACK
    for e in range(halves):
        for i in range(n):
            xi[e, i * width : (i + 1) * width, :] = x_ref[
                i, :, e * LANES : (e + 1) * LANES
            ].astype(jnp.float32)
        for c in range(width):
            xs[e, c, 0:n, :] = jnp.zeros((n, LANES), jnp.float32)
            xs[e, c, n : 2 * n, :] = xi[e, pl.ds(c, n, stride=width), :]
    lane = lax.broadcasted_iota(jnp.int32, (PACK, LANES), 1)
    sub = lax.broadcasted_iota(jnp.int32, (PACK, LANES), 0)

    def one(p, carry):
        def skewed(m):
            if m == 0:
                return jnp.zeros((PACK, LANES), jnp.float32)
            row = f_ref[p, m - 1 : m, :]
            return pltpu.roll(
                jnp.broadcast_to(row, (PACK, LANES)), 0, 1, stride=1, stride_axis=0
            )

        def turns(m, part):
            now = skewed(m)
            base = jnp.where(lane >= sub, now, part).astype(jnp.bfloat16)
            return now, [base] + [
                pltpu.roll(base, LANES - PACK * k, 1) for k in range(1, groups)
            ]

        def stack(before, after):
            tiles = [after[0]]
            for k in range(groups - 1, 0, -1):
                tiles.append(jnp.where(lane < LANES - PACK * k, before[k], after[k]))
            return jnp.concatenate(tiles, axis=0)

        part, before = turns(0, skewed(0))
        old = jnp.zeros((LANES, LANES), jnp.bfloat16)
        acc = None
        for d in range(n):
            cols = [old]
            for e in range(halves):
                part, after = turns(d * halves + e + 1, part)
                cols.append(stack(before, after))
                before = after
            old = cols[-1]
            rhs = jnp.concatenate(
                [jnp.concatenate(cols[1:], axis=1), jnp.concatenate(cols[:-1], axis=1)], axis=0
            )
            lhs = jnp.concatenate(
                [
                    jnp.concatenate(
                        [
                            xs[e, 2 * p + c, n - d : 2 * n - d, :].astype(jnp.bfloat16)
                            for e in range(halves)
                        ],
                        axis=1,
                    )
                    for c in range(2)
                ],
                axis=0,
            )
            out = jnp.dot(lhs, rhs, preferred_element_type=jnp.float32)
            acc = out if acc is None else acc + out
        for e in range(halves):
            for c in range(2):
                ys[e, pl.ds(2 * p + c, n, stride=width), :] = acc[
                    c * n : (c + 1) * n, e * LANES : (e + 1) * LANES
                ]
        return carry

    lax.fori_loop(0, width // 2, one, 0, unroll=4 if n <= 16 else 1)
    for e in range(halves):
        for i in range(n):
            y_ref[i, :, e * LANES : (e + 1) * LANES] = ys[
                e, i * width : (i + 1) * width, :
            ].astype(jnp.bfloat16)


def convolve(x, f):
    n, chans, tok = x.shape
    width = min(16, chans)
    halves = tok // LANES
    assert halves == 2
    return pl.pallas_call(
        functools.partial(conv_kernel, n, tok, width),
        grid=(chans // width,),
        in_specs=[
            pl.BlockSpec((n, width, tok), lambda g: (0, g, 0)),
            pl.BlockSpec((width // 2, n * halves, LANES), lambda g: (g, 0, 0)),
        ],
        out_specs=pl.BlockSpec((n, width, tok), lambda g: (0, g, 0)),
        out_shape=jax.ShapeDtypeStruct(x.shape, jnp.bfloat16),
        scratch_shapes=[
            pltpu.VMEM((halves, n * width, LANES), jnp.float32),
            pltpu.VMEM((halves, width, 2 * n, LANES), jnp.float32),
            pltpu.VMEM((halves, n * width, LANES), jnp.float32),
        ],
        name="convolve",
    )(x, f)


def mix(key_feat, value_feat, edges, short_filter):
    tokens, channels = key_feat.shape
    wide = min(512, channels)
    rows = pl.BlockSpec((tokens, wide), lambda g: (0, g))
    return pl.pallas_call(
        mix_kernel,
        grid=(channels // wide,),
        in_specs=[
            rows,
            rows,
            pl.BlockSpec((3, TAPS - 1, wide), lambda g: (0, 0, g)),
            pl.BlockSpec((3, TAPS, wide), lambda g: (0, 0, g)),
        ],
        out_specs=[rows, pl.BlockSpec((wide, tokens), lambda g: (g, 0))],
        out_shape=[
            jax.ShapeDtypeStruct((tokens, channels), jnp.float32),
            jax.ShapeDtypeStruct((channels, tokens), jnp.bfloat16),
        ],
        name="mix",
    )(key_feat, value_feat, edges, short_filter)


def gate(query_feat, edges, short_filter, gain, mixed, conv):
    tokens, channels = query_feat.shape
    wide = min(512, channels)
    rows = pl.BlockSpec((tokens, wide), lambda g: (0, g))
    return pl.pallas_call(
        gate_kernel,
        grid=(channels // wide,),
        in_specs=[
            rows,
            pl.BlockSpec((3, TAPS - 1, wide), lambda g: (0, 0, g)),
            pl.BlockSpec((3, TAPS, wide), lambda g: (0, 0, g)),
            pl.BlockSpec((1, wide), lambda g: (0, g)),
            rows,
            pl.BlockSpec((wide, tokens), lambda g: (g, 0)),
        ],
        out_specs=rows,
        out_shape=jax.ShapeDtypeStruct((tokens, channels), jnp.bfloat16),
        name="gate",
    )(query_feat, edges, short_filter, gain, mixed, conv)


def local(query_feat, key_feat, value_feat, short_filter, long_filter, direct_gain, out_weight):
  if True:
    tokens, channels = query_feat.shape
    devices = lax.axis_size("seq")
    sides = lax.axis_size("ch")
    with jax.named_scope("wgather"):
        weights = lax.all_gather(out_weight, "seq", axis=0, tiled=True)
    with jax.named_scope("edge"):
        last = slice(tokens - (TAPS - 1), None)
        edges = shifted(jnp.stack([query_feat[last], key_feat[last], value_feat[last]]), "seq", 1)
    with jax.named_scope("filters"):
        pairs = long_filter.shape[0] // devices
        sent = long_filter.astype(jnp.bfloat16).reshape(devices, pairs, tokens)
        taps = lax.all_to_all(sent, "seq", split_axis=0, concat_axis=0, tiled=True)
        taps = taps.astype(jnp.float32).transpose(1, 0, 2)
        taps = taps.reshape(pairs, devices * tokens // LANES, LANES)
    with jax.named_scope("mix"):
        mixed, turned = mix(key_feat, value_feat, edges, short_filter)
    with jax.named_scope("spread"):
        spread = lax.all_to_all(
            turned.reshape(devices, 2 * pairs, tokens), "seq", split_axis=0, concat_axis=0, tiled=True
        )
    with jax.named_scope("conv"):
        conv = convolve(spread, taps)
    with jax.named_scope("back"):
        long_out = lax.all_to_all(conv, "seq", split_axis=0, concat_axis=0, tiled=True)
    with jax.named_scope("gate"):
        gated = gate(query_feat, edges, short_filter, direct_gain[None], mixed, long_out.reshape(channels, tokens))
    with jax.named_scope("swap"):
        place = lax.axis_index("ch")
        pieces = [gated]
        for step in range(1, sides):
            route = [((i + step) % sides, i) for i in range(sides)]
            pieces.append(lax.ppermute(gated, "ch", route))
    with jax.named_scope("project"):
        if sides == 2:
            first = jnp.where(place == 0, pieces[0], pieces[1])
            second = jnp.where(place == 0, pieces[1], pieces[0])
            features = jnp.concatenate([first, second], axis=1)
        else:
            stacked = jnp.concatenate(pieces + pieces, axis=1)
            features = lax.dynamic_slice_in_dim(stacked, (sides - place) % sides * channels, sides * channels, 1)
        result = jnp.dot(features, weights, preferred_element_type=jnp.float32)
        return result.astype(jnp.bfloat16)


def solution(mesh):
    in_specs = (
        P("seq", "ch"),
        P("seq", "ch"),
        P("seq", "ch"),
        P(None, None, "ch"),
        P("ch", "seq"),
        P("ch"),
        P("seq", "ch"),
    )
    step = jax.shard_map(local, mesh=mesh, in_specs=in_specs, out_specs=P("seq", "ch"), check_vma=False)
    return step
```

time: 406 us -> 226 us (0.56)
  waiting for transfers between devices: 254 us -> 65.9 us
  matrix products: 73.3 us -> 9.34 us
  blocking collectives: 0 us -> 53.5 us
  Pallas kernels: 0 us -> 46.9 us
  other arithmetic: 16.2 us -> 3.58 us
  local copies, waits for them, and re-layouts: 15.5 us -> 4.79 us
    all_gather x2 -> x1, waiting for transfers between devices: 168 us -> 0.02 us  [local(): weights = lax.all_gather(out_weight, 'seq', axis=0, tiled=True)]
    dot_general x17 -> x1, matrix products: 73.3 us -> 9.34 us  [local(): result = jnp.dot(features, weights, preferred_element_type=jnp.float32)]
    all_to_all x0 -> x1, blocking collectives: none -> 53.5 us  [local(): lax.all_to_all(conv, 'seq', split_axis=0, concat_axis=0, tiled=True)]
    pallas_call x0 -> x3, Pallas kernels: none -> 46.9 us  [the longest x1 37.4 us: convolve(): pl.pallas_call(functools.partial(conv_kernel, n, tok, width), grid=(chans...]
    all_to_all x3 -> x2, waiting for transfers between devices: 85.9 us -> 40.8 us  [the longest x1 31.7 us: local(): lax.all_to_all(turned.reshape(devices, 2 * pairs, tokens), 'seq', split_a...]
    ppermute x0 -> x1, waiting for transfers between devices: none -> 23.6 us  [local(): pieces.append(lax.ppermute(gated, 'ch', route))]
    convert_element_type x4 -> x1, other arithmetic: 9.59 us -> 2.08 us  [local(): sent = long_filter.astype(jnp.bfloat16).reshape(devices, pairs, tokens)]
    unnamed x18 -> x4, local copies, waits for them, and re-layouts: 7.48 us -> 1.57 us
  transfers between devices with their start and end apart: 6 -> 5, of which waited for: 5 -> 4; matrix products, arithmetic and copies ran while one was open for 5% -> 3% of each run, Pallas kernels for 0% -> 21%
where the time goes in v1:
time: 226 us; the launch traced here: 224 us
  waiting for transfers between devices  65.9 us (29%)
  blocking collectives  53.5 us (24%)
  Pallas kernels  46.9 us (21%)
  starting transfers between devices  26.8 us (12%)
  between operations  13.5 us (6%)
  matrix products  9.34 us (4%)
  local copies, waits for them, and re-layouts  4.79 us (2%)
  other arithmetic  3.58 us (2%)
    all_to_all x1, blocking collectives, local(): lax.all_to_all(conv, 'seq', split_axis=0, concat_axis=0, tiled=True)  53.5 us
    pallas_call x1, Pallas kernels, convolve(): pl.pallas_call(functools.partial(conv_kernel, n, tok, width), grid=(chans...  37.4 us
    all_to_all x1, waiting for transfers between devices, local(): lax.all_to_all(turned.reshape(devices, 2 * pairs, tokens), 'seq', split_a...  31.7 us
    ppermute x1, waiting for transfers between devices, local(): pieces.append(lax.ppermute(gated, 'ch', route))  23.6 us
    all_to_all x1, starting transfers between devices, local(): lax.all_to_all(turned.reshape(devices, 2 * pairs, tokens), 'seq', split_a...  15.6 us
    dot_general x1, matrix products, local(): result = jnp.dot(features, weights, preferred_element_type=jnp.float32)  9.34 us
    all_to_all x1, waiting for transfers between devices, local(): taps = lax.all_to_all(sent, 'seq', split_axis=0, concat_axis=0, tiled=True)  9.09 us
    all_to_all x1, starting transfers between devices, local(): taps = lax.all_to_all(sent, 'seq', split_axis=0, concat_axis=0, tiled=True)  7.39 us
  transfers between devices with their start and end apart: 5, of which 4 were waited for; matrix products, arithmetic and copies ran while one was open for 3% of the time, Pallas kernels for 21%

profile of v1, /device:TPU:0, one launch (start us, length us, event | category | flops | bytes accessed | tf_op | source)
XLA Modules:
  0.0 224.4 jit_solution(16780228487875390170)
XLA Ops:
  6.5 0.7 all-gather.2.cloned.1.call-update
  7.3 2.1 convert_element_type.7
  9.3 7.4 %all-to-all-start.1 = ((bf16[16,64,256]{2,1,0:T(8,128)(2,1)}), bf16[16,64,256]{2,1,0:T(8,128)(2,1)S(1)}, u32[]{:S(2)}, u32[]{:S(2)}) async-start(bf16[16,64,256]{2,1,0:T(8,128)(2,1)} %bitcast.5), calls=%async_computation.1 | async-start | bytes 1048576 | tf_op jit(solution)/shard_map/filters/all_to_all | solution.py:209
  16.7 0.8 slice_bitcast_fusion.2
  17.5 0.8 slice_bitcast_fusion
  18.4 2.3 %collective-permute-start = (bf16[3,2,2048]{2,1,0:T(2,128)(2,1)S(1)}, bf16[3,2,2048]{2,1,0:T(2,128)(2,1)S(1)}, u32[]{:S(2)}, u32[]{:S(2)}) collective-permute-start(bf16[3,2,2048]{2,1,0:T(2,128)(2,1)S(1)} %pad_maximum_fusion), channel_id=1, source_target_pairs={{0,2},{2,4},{4,6},{6,8},{8,10},{10,12},{12,14},{14,16},{16,18},{18... | collective-permute-start | bytes 73736 | tf_op jit(solution)/shard_map/edge/ppermute | solution.py:19
  20.7 0.8 collective-permute-done.edge_ref
  21.5 0.6 copy-done.1
  22.1 4.7 %mix.1 = (f32[256,2048]{1,0:T(8,128)}, bf16[2048,256]{1,0:T(8,128)(2,1)}) custom-call(bf16[256,2048]{1,0:T(8,128)(2,1)} %key_ref.1, bf16[256,2048]{1,0:T(8,128)(2,1)} %value_ref.1, bf16[3,2,2048]{2,1,0:T(2,128)(2,1)} %copy-done.1, f32[3,3,2048]{2,1,0:T(4,128)} %short_ref.3), custom_call_target="tpu_custom_call" | custom-call | tf_op jit(solution)/shard_map/mix/mix/pallas_call | solution.py:157
  26.8 9.1 %all-to-all-done.1 = bf16[16,64,256]{2,1,0:T(8,128)(2,1)S(1)} async-done(((bf16[16,64,256]{2,1,0:T(8,128)(2,1)}), bf16[16,64,256]{2,1,0:T(8,128)(2,1)S(1)}, u32[]{:S(2)}, u32[]{:S(2)}) %all-to-all-start.1) | async-done | bytes 524320 | tf_op jit(solution)/shard_map/filters/all_to_all | solution.py:209
  35.9 15.6 %all-to-all-start = ((bf16[16,128,256]{2,1,0:T(8,128)(2,1)}), bf16[16,128,256]{2,1,0:T(8,128)(2,1)S(1)}, u32[]{:S(2)}, u32[]{:S(2)}) async-start(bf16[16,128,256]{2,1,0:T(8,128)(2,1)} %bitcast.14), calls=%async_computation | async-start | bytes 2097152 | tf_op jit(solution)/shard_map/spread/all_to_all | solution.py:215
  51.5 0.1 convert_bitcast_fusion
  51.6 0.6 copy.9
  52.2 1.0 reshape.20.f_ref
  53.3 31.7 %all-to-all-done.x_ref = bf16[16,128,256]{2,1,0:T(8,128)(2,1)S(1)} async-done(((bf16[16,128,256]{2,1,0:T(8,128)(2,1)}), bf16[16,128,256]{2,1,0:T(8,128)(2,1)S(1)}, u32[]{:S(2)}, u32[]{:S(2)}) %all-to-all-start) | async-done | bytes 1048608 | tf_op jit(solution)/shard_map/spread/all_to_all | solution.py:215
  85.0 1.0 copy-done
  85.9 37.4 %convolve.1 = bf16[16,128,256]{2,1,0:T(8,128)(2,1)} custom-call(bf16[16,128,256]{2,1,0:T(8,128)(2,1)} %copy-done, f32[64,32,128]{2,1,0:T(8,128)} %reshape.20.f_ref), custom_call_target="tpu_custom_call" | custom-call | tf_op jit(solution)/shard_map/conv/convolve/pallas_call | solution.py:135
  123.4 53.5 %all_to_all.15 = bf16[16,128,256]{2,1,0:T(8,128)(2,1)} all-to-all(bf16[16,128,256]{2,1,0:T(8,128)(2,1)} %convolve.1), channel_id=1, replica_groups=mesh['seq'=16,'ch'=2] {'seq'}, dimensions={0} | all-to-all | bytes 2097152 | tf_op jit(solution)/shard_map/back/all_to_all | solution.py:221
  176.9 4.8 %gate.1 = bf16[256,2048]{1,0:T(8,128)(2,1)} custom-call(bf16[256,2048]{1,0:T(8,128)(2,1)} %query_ref.1, bf16[3,2,2048]{2,1,0:T(2,128)(2,1)} %copy-done.1, f32[3,3,2048]{2,1,0:T(4,128)} %short_ref.3, f32[1,2048]{1,0:T(1,128)} %bitcast.15, f32[256,2048]{1,0:T(8,128)} %get-tuple-element.7.mixed_ref, bf16[2048,256]{1,0:T(8,128)(2,1)} %bitcast.13), custom_call_target="tpu_custom_call" | custom-call | tf_op jit(solution)/shard_map/gate/gate/pallas_call | solution.py:179
  181.7 1.5 collective-permute-start.1
  183.2 23.6 %collective-permute-done.1 = bf16[256,2048]{1,0:T(8,128)(2,1)S(1)} collective-permute-done((bf16[256,2048]{1,0:T(8,128)(2,1)}, bf16[256,2048]{1,0:T(8,128)(2,1)S(1)}, u32[]{:S(2)}, u32[]{:S(2)}) %collective-permute-start.1) | collective-permute-done | bytes 1048608 | tf_op jit(solution)/shard_map/swap/ppermute | solution.py:229
  206.8 1.4 broadcast_select_fusion.1
  208.2 0.0 all-gather.2.cloned.1.call-done
  208.2 9.3 %convolution_convert_fusion = bf16[256,2048]{1,0:T(8,128)(2,1)} fusion(bf16[4096,2048]{1,0:T(8,128)(2,1)} %all-gather.2.cloned.1.call-done, bf16[256,2048]{1,0:T(8,128)(2,1)S(1)} %get-tuple-element.10, bf16[256,2048]{1,0:T(8,128)(2,1)S(1)} %get-tuple-element.9), kind=kOutput, calls=%fused_computation | convolution fusion | flops 4299685888 | bytes 19922944 | tf_op jit(solution)/shard_map/project/dot_general | solution.py:238
  (4 shorter events, 0.0 us)
Async XLA Ops:
  6.5 201.7 %all-gather.2.cloned.1.call-start = ((), (), s32[]{:S(2)}) async-start(), calls=%async_computation.3 | async-start | bytes 17825792 | tf_op jit(solution)/shard_map/wgather/all_gather | solution.py:202
  9.3 26.6 %all-to-all-start.1 = ((bf16[16,64,256]{2,1,0:T(8,128)(2,1)}), bf16[16,64,256]{2,1,0:T(8,128)(2,1)S(1)}, u32[]{:S(2)}, u32[]{:S(2)}) async-start(bf16[16,64,256]{2,1,0:T(8,128)(2,1)} %bitcast.5), calls=%async_computation.1 | async-start | bytes 1048576 | tf_op jit(solution)/shard_map/filters/all_to_all | solution.py:209
  18.4 3.1 %collective-permute-start = (bf16[3,2,2048]{2,1,0:T(2,128)(2,1)S(1)}, bf16[3,2,2048]{2,1,0:T(2,128)(2,1)S(1)}, u32[]{:S(2)}, u32[]{:S(2)}) collective-permute-start(bf16[3,2,2048]{2,1,0:T(2,128)(2,1)S(1)} %pad_maximum_fusion), channel_id=1, source_target_pairs={{0,2},{2,4},{4,6},{6,8},{8,10},{10,12},{12,14},{14,16},{16,18},{18... | collective-permute-start | bytes 73736 | tf_op jit(solution)/shard_map/edge/ppermute | solution.py:19
  21.5 0.6 copy-start.1
  35.9 49.0 %all-to-all-start = ((bf16[16,128,256]{2,1,0:T(8,128)(2,1)}), bf16[16,128,256]{2,1,0:T(8,128)(2,1)S(1)}, u32[]{:S(2)}, u32[]{:S(2)}) async-start(bf16[16,128,256]{2,1,0:T(8,128)(2,1)} %bitcast.14), calls=%async_computation | async-start | bytes 2097152 | tf_op jit(solution)/shard_map/spread/all_to_all | solution.py:215
  85.0 1.0 copy-start
  181.7 25.1 %collective-permute-start.1 = (bf16[256,2048]{1,0:T(8,128)(2,1)}, bf16[256,2048]{1,0:T(8,128)(2,1)S(1)}, u32[]{:S(2)}, u32[]{:S(2)}) collective-permute-start(bf16[256,2048]{1,0:T(8,128)(2,1)} %gate.1), channel_id=1, source_target_pairs={{1,0},{0,1},{3,2},{2,3},{5,4},{4,5},{7,6},{6,7},{9,8},{8,9},{11,10... | collective-permute-start | bytes 3145736 | tf_op jit(solution)/shard_map/swap/ppermute | solution.py:229
Sparse Core Ops, SparseCore 0:
  9.5 174.7 all-gather.1
